TPU v7x, 128 devices: a whole 4x4x4 slice. The times are simulated.
128 devices in a mesh: req: 32 (over z, y, x_hi), tensor: 4 (over x_lo, core).
Axes of the slice: x: 4 (x_hi: 2, x_lo: 2; x = x_hi * 2 + x_lo), y: 4, z: 4, core: 2. Of those that a mesh axis runs over, the one named last changes fastest.
Arguments:
- span_in: bfloat16 [64, 512, 2048], P('req'), may hold values from -6 to 6
- w_qkv: bfloat16 [3, 2048, 2048], P(None, None, 'tensor'), may hold values from -1 to 1
- qk_gain: bfloat16 [2, 2048], P(None, 'tensor'), may hold values from 0.099609375 to 1.8984375
- w_out: bfloat16 [2048, 2048], P('tensor'), may hold values from -1 to 1
- post_gain: bfloat16 [2048], P('tensor'), may hold values from 0.099609375 to 1.8984375
- kv_pool: bfloat16 [4, 2048, 16, 2048], P(None, 'req', None, 'tensor'), may hold values from -66 to 66
- block_table: int32 [64, 32], replicated, may hold values from 0 to 63, as said below
- request_order: int32 [64], replicated, may hold values from 0 to 63, each once
- lengths: int32 [64], replicated, may hold values from 1 to 512, as said below
Outputs:
- span_out: bfloat16 [64, 512, 2048], P('req', None, 'tensor')
- relaid_cache: bfloat16 [4, 64, 512, 2048], P(None, 'req', None, 'tensor')
Inputs may be any that keep to these rules, and one draw needn't show every extreme that they name: `block_table`: entry (r, j) is the slot, among the 64 slots of the req index j modulo the number of req devices, that holds block j of request r; each slot of each req index is named once. `lengths`: some request has exactly 512 cached tokens.
All inputs are finite; a program needn't handle non-finite values.
Results may differ from a plain program's by a relative error of at most 0.0095.
Values may be sent and summed in bfloat16 or wider, within the bound.
A program may use at most 192 MiB of HBM per device.

v0:
```python
import jax
import jax.numpy as jnp
from jax import lax
from jax.sharding import PartitionSpec as P

HD = 128
norm_eps = 1e-06
rope_base = 500000.0


def rotate(values, positions):
    half_dim = values.shape[-1] // 2
    frequency = rope_base ** (-jnp.arange(half_dim, dtype=jnp.float32) * (2.0 / values.shape[-1]))
    angles = positions[:, None] * frequency[None, :]
    cosine = jnp.cos(angles)[:, None, :]
    sine_part = jnp.sin(angles)[:, None, :]
    first_half = values[..., :half_dim]
    second_half = values[..., half_dim:]
    return jnp.concatenate(
        [
            first_half * cosine - second_half * sine_part,
            second_half * cosine + first_half * sine_part,
        ],
        axis=-1,
    )


def on_device(
    span_in, w_qkv, qk_gain, w_out, post_gain, kv_pool, block_table, request_order, lengths
):
    req_count = lax.axis_size("req")
    req_index = lax.axis_index("req")
    per_device = span_in.shape[0]
    span_len = span_in.shape[1]
    full_width = span_in.shape[2]
    part_width = w_qkv.shape[2]
    block_len = kv_pool.shape[2]
    blocks_each = block_table.shape[1] // req_count
    wanted = jnp.transpose(request_order.reshape(req_count, per_device))
    table_rows = jnp.take(block_table, wanted, axis=0)
    local_blocks = req_index + req_count * jnp.arange(blocks_each, dtype=jnp.int32)
    picked = jnp.take(table_rows, local_blocks, axis=2)
    picked = jnp.transpose(picked, (0, 2, 1)).reshape(-1)
    gathered = jnp.take(kv_pool, picked, axis=1)
    received = lax.all_to_all(
        gathered.reshape(
            kv_pool.shape[0], per_device, blocks_each, req_count * block_len, part_width
        ),
        "req",
        split_axis=3,
        concat_axis=3,
        tiled=True,
    )
    relaid = received.reshape(kv_pool.shape[0], per_device, -1, part_width)
    my_order = lax.dynamic_slice_in_dim(request_order, req_index * per_device, per_device)
    my_lengths = jnp.take(lengths, my_order)
    flat_in = span_in.reshape(-1, full_width)
    projected = jnp.einsum("rd,mdw->mrw", flat_in, w_qkv, preferred_element_type=jnp.float32)
    queries = projected[0]
    keys_new = projected[1]
    values_new = projected[2].astype(jnp.bfloat16)
    query_sq, key_sq = lax.psum(
        (jnp.sum(queries * queries, axis=-1), jnp.sum(keys_new * keys_new, axis=-1)), "tensor"
    )
    norm_gains = qk_gain.astype(jnp.float32)
    queries = queries * lax.rsqrt(query_sq / full_width + norm_eps)[:, None] * norm_gains[0]
    keys_new = keys_new * lax.rsqrt(key_sq / full_width + norm_eps)[:, None] * norm_gains[1]
    positions = (
        my_lengths.astype(jnp.float32)[:, None] + jnp.arange(span_len, dtype=jnp.float32)[None, :]
    ).reshape(-1)
    local_heads = part_width // HD
    query_rot = rotate(queries.reshape(-1, local_heads, HD), positions).astype(jnp.bfloat16)
    query_rot = query_rot.reshape(per_device, span_len, local_heads, HD)
    key_rot = rotate(keys_new.reshape(-1, local_heads, HD), positions).astype(jnp.bfloat16)
    key_rot = key_rot.reshape(per_device, span_len, local_heads, HD)
    context = relaid.shape[2]
    all_keys = jnp.concatenate(
        [relaid[0].reshape(per_device, context, local_heads, HD), key_rot], axis=1
    )
    all_values = jnp.concatenate(
        [
            relaid[1].reshape(per_device, context, local_heads, HD),
            values_new.reshape(per_device, span_len, local_heads, HD),
        ],
        axis=1,
    )
    scores = jnp.einsum(
        "bqhd,bkhd->bhqk", query_rot, all_keys, preferred_element_type=jnp.float32
    ) * HD ** (-0.5)
    cache_live = jnp.arange(context, dtype=jnp.int32)[None, :] < my_lengths[:, None]
    causal = jnp.arange(span_len)[None, :] <= jnp.arange(span_len)[:, None]
    live_mask = jnp.concatenate(
        [
            jnp.broadcast_to(cache_live[:, None, :], (per_device, span_len, context)),
            jnp.broadcast_to(causal[None], (per_device, span_len, span_len)),
        ],
        axis=2,
    )
    scores = jnp.where(live_mask[:, None], scores, -1e30)
    maxima = jnp.max(scores, axis=-1, keepdims=True)
    exponent = jnp.exp(scores - maxima)
    weights = (exponent / jnp.sum(exponent, axis=-1, keepdims=True)).astype(jnp.bfloat16)
    attended = jnp.einsum(
        "bhqk,bkhd->bqhd", weights, all_values, preferred_element_type=jnp.float32
    )
    attended = attended.astype(jnp.bfloat16).reshape(-1, part_width)
    partial_value = jnp.dot(attended, w_out, preferred_element_type=jnp.float32)
    tensor_index = lax.axis_index("tensor")
    residual_part = lax.dynamic_slice_in_dim(
        flat_in, tensor_index * part_width, part_width, 1
    ).astype(jnp.float32)
    gain_part = post_gain.astype(jnp.float32)
    summed = lax.psum(partial_value.astype(jnp.bfloat16), "tensor").astype(jnp.float32)
    scale_rows = lax.rsqrt(jnp.mean(summed * summed, axis=-1, keepdims=True) + norm_eps)
    own_share = lax.dynamic_slice_in_dim(summed, tensor_index * part_width, part_width, 1)
    layer_out = (residual_part + own_share * scale_rows * gain_part).astype(jnp.bfloat16)
    return (layer_out.reshape(per_device, span_len, part_width), relaid)


def solution(mesh):
    placed = (
        P("req", None, None),
        P(None, None, "tensor"),
        P(None, "tensor"),
        P("tensor", None),
        P("tensor"),
        P(None, "req", None, "tensor"),
        P(),
        P(),
        P(),
    )
    return jax.shard_map(
        on_device,
        mesh=mesh,
        in_specs=placed,
        out_specs=(P("req", None, "tensor"), P(None, "req", None, "tensor")),
        check_vma=False,
    )
```

profile of v0, /device:TPU:1, one launch (start us, length us, event | category | flops | bytes accessed | tf_op | source)
XLA Modules:
  0.0 270.8 jit_solution(14465095064436898901)
XLA Ops:
  7.2 0.9 reshape.246
  8.1 0.1 copy.77
  8.2 0.1 copy.78
  8.3 0.1 reshape.292
  8.4 0.8 copy.79
  9.2 0.6 gather_fusion
  9.8 0.1 constant_dynamic-slice_fusion
  9.9 0.1 copy.100
  10.0 0.1 select_n.95
  10.1 0.1 copy.81
  10.2 0.1 copy.84
  10.3 0.1 broadcast_in_dim.91
  10.3 0.1 broadcast_in_dim.92
  10.5 5.0 %gather_fusion.1 = bf16[64,4,16,512]{3,2,1,0:T(8,128)(2,1)} fusion(bf16[4,64,16,512]{3,2,1,0:T(8,128)(2,1)} %param.14, s32[1024]{0:T(1024)S(1)} %pad_clamp_fusion.1), kind=kCustom, calls=%fused_computation.1 | custom fusion | bytes 8388864 | tf_op jit(solution)/shard_map/jit(_take)/gather | solution.py:44
  15.5 2.6 copy.85
  18.1 0.5 broadcast_select_fusion
  18.6 6.3 %copy.86 = bf16[4,2,1,512,512]{4,1,0,2,3:T(2,128)(2,1)} copy(bf16[4,2,1,512,512]{4,3,1,0,2:T(8,128)(2,1)S(1)} %broadcast_select_fusion) | data formatting | bytes 8388608 | tf_op jit(solution)/shard_map/jit(_take)/select_n | solution.py:44
  24.9 11.6 %all-to-all-start = ((bf16[4,2,1,512,512]{4,1,0,2,3:T(2,128)(2,1)}), bf16[4,2,1,512,512]{4,1,0,2,3:T(2,128)(2,1)}, u32[]{:S(2)}, u32[]{:S(2)}) async-start(bf16[4,2,1,512,512]{4,1,0,2,3:T(2,128)(2,1)} %copy.86), calls=%async_computation | async-start | bytes 8388608 | tf_op jit(solution)/shard_map/all_to_all | solution.py:45
  36.5 0.0 all-reduce.3.cloned.1.call-start
  36.6 0.1 compare_select_fusion.2
  36.7 0.6 gather_fusion.2
  37.3 0.1 fusion.31
  37.4 0.1 add_bitcast_fusion
  37.5 10.1 %convolution_bitcast_fusion = f32[3,1024,512]{1,2,0:T(8,128)S(1)} fusion(bf16[3,2048,512]{2,1,0:T(8,128)(2,1)} %param.10, bf16[1024,2048,1]{1,0,2:T(8,128)(2,1)} %bitcast.59), kind=kOutput, calls=%fused_computation.16 | convolution fusion | flops 6442450944 | bytes 16777216 | tf_op jit(solution)/shard_map/rd,mdw->mrw/dot_general | solution.py:58
  47.6 2.6 copy-done.4
  50.2 1.1 slice.84
  51.3 1.8 convert_element_type.42
  53.2 1.1 copy.89
  54.3 5.0 %multiply_reduce_fusion.2 = (f32[1024]{0:T(1024)S(1)}, f32[1024]{0:T(1024)S(1)}, f32[1,1024,512]{1,2,0:T(8,128)}, f32[1,1024,512]{1,2,0:T(8,128)}) fusion(f32[3,1024,512]{1,2,0:T(8,128)} %copy-done.4), kind=kLoop, calls=%fused_computation.31 | loop fusion | flops 2095104 | bytes 8396800 | tf_op jit(solution)/shard_map/reduce_sum | solution.py:63
  59.4 32.4 %all-reduce = (f32[1024]{0:T(1024)S(1)}, f32[1024]{0:T(1024)S(1)}) all-reduce(f32[1024]{0:T(1024)S(1)} %get-tuple-element.18, f32[1024]{0:T(1024)S(1)} %get-tuple-element.17), channel_id=1, replica_groups=mesh['req'=32,'tensor'=4] {'tensor'}, use_global_device_ids=true, to_apply=%region_3.4 | all-reduce | flops 2048 | bytes 16384 | tf_op jit(solution)/shard_map/psum | solution.py:62
  91.8 1.0 multiply_cosine_fusion
  92.8 1.8 multiply_multiply_fusion.1
  94.6 0.2 multiply_multiply_fusion
  94.9 1.9 subtract_convert_fusion.1
  96.8 1.4 concatenate.29
  98.2 1.4 copy.90
  99.6 1.4 concatenate.30
  101.0 1.4 copy.91
  102.4 1.4 concatenate.33
  103.8 1.3 copy.94
  105.1 0.4 concatenate.32
  105.5 1.4 copy.93
  106.9 0.1 iota_compare_fusion
  107.0 0.1 iota_compare_fusion.1
  107.0 0.1 broadcast_in_dim.97
  107.2 0.1 broadcast_in_dim.96
  107.3 1.1 pad_add_fusion
  108.4 3.5 %fusion.32 = (bf16[1,2,1,512,512]{4,1,0,2,3:T(2,128)(2,1)S(1)}, bf16[1,2,1,512,512]{4,1,0,2,3:T(2,128)(2,1)}) fusion(bf16[4,2,1,512,512]{4,1,0,2,3:T(2,128)(2,1)} %all-to-all-done), kind=kLoop, calls=%fused_computation.70 | loop fusion | bytes 4194304 | tf_op jit(solution)/shard_map/slice | solution.py:82
  111.9 2.5 copy.87
  114.3 2.4 copy.99
  116.8 1.3 copy.95
  118.1 10.6 %fusion.9 = f32[2,4,512,1024]{3,2,1,0:T(8,128)} fusion(bf16[2,512,4,64]{3,1,2,0:T(8,128)(2,1)} %copy.94, bf16[2,512,4,64]{3,1,2,0:T(8,128)(2,1)} %copy.93, bf16[2,512,4,128]{3,1,2,0:T(8,128)(2,1)} %copy.95, bf16[2,512,4,64]{3,1,2,0:T(8,128)(2,1)} %copy.91, bf16[2,512,4,64]{3,1,2,0:T(8,128)(2,1)} %copy.90), kind=kOutput, calls=%fused_computation.21 | convolution fusion | flops 1082130432 | bytes 19922944 | tf_op jit(solution)/shard_map/bqhd,bkhd->bhqk/dot_general | solution.py:87
  128.7 22.1 %fusion.34 = (f32[2,4,512]{2,1,0:T(4,128)S(1)}, f32[2,4,512,1024]{3,2,1,0:T(8,128)}) fusion(f32[2,4,512,1024]{3,2,1,0:T(8,128)} %fusion.9, pred[2,512,1024]{2,1,0:T(8,128)(4,1)} %pad_add_fusion), kind=kOutput, calls=%fused_computation.72 | output fusion | flops 25166848 | bytes 34619392 | tf_op jit(solution)/shard_map/sub | solution.py:101
  150.8 8.5 %fusion.18 = bf16[2,512,4,128]{1,3,2,0:T(8,128)(2,1)} fusion(f32[2,4,512,1024]{3,2,1,0:T(8,128)} %get-tuple-element.38, f32[2,4,512]{2,1,0:T(4,128)S(1)} %get-tuple-element.37, bf16[2,512,4,128]{1,3,2,0:T(8,128)(2,1)S(1)} %copy-done.5, bf16[2,512,4,128]{1,3,2,0:T(8,128)(2,1)} %bitcast.57), kind=kOutput, calls=%fused_computation.33 | convolution fusion | flops 1086849024 | bytes 19939328 | tf_op jit(solution)/shard_map/bhqk,bkhd->bqhd/dot_general | solution.py:103
  159.3 1.7 copy.96
  161.0 4.3 %convolution_convert_fusion = bf16[1024,2048]{1,0:T(8,128)(2,1)} fusion(bf16[512,2048]{1,0:T(8,128)(2,1)S(1)} %copy-done, bf16[128,8,4,128]{3,2,1,0:T(4,128)(2,1)S(1)} %bitcast.58), kind=kOutput, calls=%fused_computation.15 | convolution fusion | flops 2149580800 | bytes 7340032 | tf_op jit(solution)/shard_map/dot_general | solution.py:107
  165.4 0.0 all-reduce.3.cloned.1.call-update
  165.4 0.6 copy-done.8
  166.0 5.7 %copy.97 = bf16[4,2,512,512]{3,2,1,0:T(8,128)(2,1)} copy(bf16[4,2,512,512]{3,1,0,2:T(2,128)(2,1)} %bitcast.20) | data formatting | bytes 8388608
  171.7 85.1 %all-reduce.3.cloned.1.call-done = bf16[1024,2048]{1,0:T(8,128)(2,1)} async-done(((bf16[1024,2048]{1,0:T(8,128)(2,1)}), bf16[1024,2048]{1,0:T(8,128)(2,1)}) %all-reduce.3.cloned.1.call-update) | async-done | bytes 4194320 | tf_op jit(solution)/shard_map/psum | solution.py:113
  256.8 3.2 %multiply_reduce_fusion = f32[1024]{0:T(1024)S(1)} fusion(bf16[1024,2048]{1,0:T(8,128)(2,1)} %all-reduce.3.cloned.1.call-done), kind=kLoop, calls=%fused_computation.8 | loop fusion | flops 6290432 | bytes 4198400 | tf_op jit(solution)/shard_map/reduce_sum | solution.py:114
  260.1 0.2 copy-done.2
  260.3 1.1 convert_element_type.49
  261.4 2.6 add_convert_fusion
  (30 shorter events, 0.1 us)
Async XLA Ops:
  7.2 153.9 %copy-start = (bf16[512,2048]{1,0:T(8,128)(2,1)S(1)}, bf16[512,2048]{1,0:T(8,128)(2,1)}, u32[]{:S(2)}) copy-start(bf16[512,2048]{1,0:T(8,128)(2,1)} %param.12) | copy-start | bytes 6291460
  24.9 11.7 %copy-start.7 = (s32[64]{0:T(128)S(1)}, s32[64]{0:T(128)}, u32[]{:S(2)}) copy-start(s32[64]{0:T(128)} %param.16) | copy-start | bytes 772
  24.9 11.8 %copy-start.1 = (s32[64]{0:T(128)S(1)}, s32[64]{0:T(128)}, u32[]{:S(2)}) copy-start(s32[64]{0:T(128)} %param.17) | copy-start | bytes 772
  24.9 83.5 %all-to-all-start = ((bf16[4,2,1,512,512]{4,1,0,2,3:T(2,128)(2,1)}), bf16[4,2,1,512,512]{4,1,0,2,3:T(2,128)(2,1)}, u32[]{:S(2)}, u32[]{:S(2)}) async-start(bf16[4,2,1,512,512]{4,1,0,2,3:T(2,128)(2,1)} %copy.86), calls=%async_computation | async-start | bytes 8388608 | tf_op jit(solution)/shard_map/all_to_all | solution.py:45
  36.5 220.3 %all-reduce.3.cloned.1.call-start = ((), (), s32[]{:S(2)}) async-start(), calls=%async_computation.1 | async-start | bytes 8388608 | tf_op jit(solution)/shard_map/psum | solution.py:113
  47.6 2.6 copy-start.4
  54.3 37.4 %copy-start.6 = (bf16[2,512]{1,0:T(2,128)(2,1)S(1)}, bf16[2,512]{1,0:T(2,128)(2,1)}, u32[]{:S(2)}) copy-start(bf16[2,512]{1,0:T(2,128)(2,1)} %param.11) | copy-start | bytes 6148
  91.7 2.9 %copy-start.3 = (f32[1,1024,512]{1,2,0:T(8,128)S(1)}, f32[1,1024,512]{1,2,0:T(8,128)}, u32[]{:S(2)}) copy-start(f32[1,1024,512]{1,2,0:T(8,128)} %get-tuple-element.24) | copy-start | bytes 6291460
  128.7 22.1 %copy-start.5 = (bf16[2,512,4,128]{1,3,2,0:T(8,128)(2,1)S(1)}, bf16[2,512,4,128]{1,3,2,0:T(8,128)(2,1)}, u32[]{:S(2)}) copy-start(bf16[2,512,4,128]{1,3,2,0:T(8,128)(2,1)} %copy.89) | copy-start | bytes 3145732
  165.4 0.7 copy-start.8
  256.8 3.4 %copy-start.2 = (bf16[1024,2048]{1,0:T(8,128)(2,1)S(1)}, bf16[1024,2048]{1,0:T(8,128)(2,1)}, u32[]{:S(2)}) copy-start(bf16[1024,2048]{1,0:T(8,128)(2,1)} %all-reduce.3.cloned.1.call-done) | copy-start | bytes 12582916
Sparse Core Ops, SparseCore 0:
  165.5 91.2 all-reduce.2
where the time goes:
time: 271 us
  waiting for transfers between devices  85.2 us (31%)
  local copies, waits for them, and re-layouts  52.8 us (19%)
  other arithmetic  41 us (15%)
  matrix products  33.6 us (12%)
  blocking collectives  32.4 us (12%)
  between operations  14.3 us (5%)
  starting transfers between devices  11.6 us (4%)
    psum x1, waiting for transfers between devices, on_device(): lax.psum(partial_value.astype(jnp.bfloat16), 'tensor').astype(jnp.float32)  85.1 us
    psum x1, blocking collectives, on_device(): lax.psum((jnp.sum(queries * queries, axis=-1), jnp.sum(keys_new * keys_ne...  32.4 us
    sub x1, other arithmetic, on_device(): exponent = jnp.exp(scores - maxima)  22.1 us
    unnamed x23, local copies, waits for them, and re-layouts  12.5 us
    all_to_all x1, starting transfers between devices, on_device(): lax.all_to_all(gathered.reshape(kv_pool.shape[0], per_device, blocks_each...  11.6 us
    dot_general x1, matrix products, on_device(): jnp.einsum('bqhd,bkhd->bhqk', query_rot, all_keys, preferred_element_type...  10.6 us
    dot_general x1, matrix products, on_device(): jnp.einsum('rd,mdw->mrw', flat_in, w_qkv, preferred_element_type=jnp.floa...  10.1 us
    concatenate x8, local copies, waits for them, and re-layouts, rotate(): jnp.concatenate([first_half * cosine - second_half * sine_part, second_ha...  10 us
  transfers between devices with their start and end apart: 2, of which 1 were waited for; matrix products, arithmetic and copies ran while one was open for 16% of the time, Pallas kernels for 0%

commit v1 on v0

--- a/solution.py
+++ b/solution.py
@@ -2,6 +2,7 @@
 import jax.numpy as jnp
 from jax import lax
 from jax.sharding import PartitionSpec as P
+from jax.lax import all_gather
 
 HD = 128
 norm_eps = 1e-06
@@ -110,7 +111,12 @@
         flat_in, tensor_index * part_width, part_width, 1
     ).astype(jnp.float32)
     gain_part = post_gain.astype(jnp.float32)
-    summed = lax.psum(partial_value.astype(jnp.bfloat16), "tensor").astype(jnp.float32)
+
+    def fields_supply_all(arr):
+        outcome_arr = jnp.sum(all_gather(arr, "tensor"), axis=0)
+        return outcome_arr
+
+    summed = fields_supply_all(partial_value.astype(jnp.bfloat16)).astype(jnp.float32)
     scale_rows = lax.rsqrt(jnp.mean(summed * summed, axis=-1, keepdims=True) + norm_eps)
     own_share = lax.dynamic_slice_in_dim(summed, tensor_index * part_width, part_width, 1)
     layer_out = (residual_part + own_share * scale_rows * gain_part).astype(jnp.bfloat16)

time: 271 us -> 343 us (1.27)
  waiting for transfers between devices: 85.2 us -> 145 us
  other arithmetic: 41 us -> 53 us
    all_gather x0 -> x1, waiting for transfers between devices: none -> 145 us  [fields_supply_all(): outcome_arr = jnp.sum(all_gather(arr, 'tensor'), axis=0)]
    psum x1 -> x0, waiting for transfers between devices: 85.1 us -> none  [on_device(): lax.psum(partial_value.astype(jnp.bfloat16), 'tensor').astype(jnp.float32)]
    reduce_sum x0 -> x1, other arithmetic: none -> 12 us  [fields_supply_all(): outcome_arr = jnp.sum(all_gather(arr, 'tensor'), axis=0)]
  transfers between devices with their start and end apart: 2 -> 2, of which waited for: 1 -> 1; matrix products, arithmetic and copies ran while one was open for 16% -> 12% of each run, Pallas kernels for 0% -> 0%
where the time goes in v1:
time: 343 us
  waiting for transfers between devices  145 us (42%)
  other arithmetic  53 us (15%)
  local copies, waits for them, and re-layouts  52.8 us (15%)
  matrix products  33.5 us (10%)
  blocking collectives  32.4 us (9%)
  between operations  14.3 us (4%)
  starting transfers between devices  11.6 us (3%)
    all_gather x1, waiting for transfers between devices, fields_supply_all(): outcome_arr = jnp.sum(all_gather(arr, 'tensor'), axis=0)  145 us
    psum x1, blocking collectives, on_device(): lax.psum((jnp.sum(queries * queries, axis=-1), jnp.sum(keys_new * keys_ne...  32.4 us
    sub x1, other arithmetic, on_device(): exponent = jnp.exp(scores - maxima)  22.1 us
    unnamed x23, local copies, waits for them, and re-layouts  12.6 us
    reduce_sum x1, other arithmetic, fields_supply_all(): outcome_arr = jnp.sum(all_gather(arr, 'tensor'), axis=0)  12 us
    all_to_all x1, starting transfers between devices, on_device(): lax.all_to_all(gathered.reshape(kv_pool.shape[0], per_device, blocks_each...  11.6 us
    dot_general x1, matrix products, on_device(): jnp.einsum('bqhd,bkhd->bhqk', query_rot, all_keys, preferred_element_type...  10.6 us
    dot_general x1, matrix products, on_device(): jnp.einsum('rd,mdw->mrw', flat_in, w_qkv, preferred_element_type=jnp.floa...  10.1 us
  transfers between devices with their start and end apart: 2, of which 1 were waited for; matrix products, arithmetic and copies ran while one was open for 12% of the time, Pallas kernels for 0%

profile of v1, /device:TPU:1, one launch (start us, length us, event | category | flops | bytes accessed | tf_op | source)
XLA Modules:
  0.0 342.5 jit_solution(1354265447396721570)
XLA Ops:
  7.2 0.9 reshape.246
  8.1 0.1 copy.77
  8.2 0.1 copy.78
  8.3 0.1 reshape.292
  8.4 0.8 copy.79
  9.2 0.6 gather_fusion
  9.8 0.1 constant_dynamic-slice_fusion
  9.9 0.1 copy.100
  10.0 0.1 select_n.95
  10.1 0.1 copy.81
  10.2 0.1 copy.84
  10.3 0.1 broadcast_in_dim.91
  10.3 0.1 broadcast_in_dim.92
  10.5 5.0 %gather_fusion.1 = bf16[64,4,16,512]{3,2,1,0:T(8,128)(2,1)} fusion(bf16[4,64,16,512]{3,2,1,0:T(8,128)(2,1)} %param.14, s32[1024]{0:T(1024)S(1)} %pad_clamp_fusion.1), kind=kCustom, calls=%fused_computation.1 | custom fusion | bytes 8388864 | tf_op jit(solution)/shard_map/jit(_take)/gather | solution.py:45
  15.5 2.6 copy.85
  18.1 0.5 broadcast_select_fusion
  18.6 6.3 %copy.86 = bf16[4,2,1,512,512]{4,1,0,2,3:T(2,128)(2,1)} copy(bf16[4,2,1,512,512]{4,3,1,0,2:T(8,128)(2,1)S(1)} %broadcast_select_fusion) | data formatting | bytes 8388608 | tf_op jit(solution)/shard_map/jit(_take)/select_n | solution.py:45
  24.9 11.6 %all-to-all-start = ((bf16[4,2,1,512,512]{4,1,0,2,3:T(2,128)(2,1)}), bf16[4,2,1,512,512]{4,1,0,2,3:T(2,128)(2,1)}, u32[]{:S(2)}, u32[]{:S(2)}) async-start(bf16[4,2,1,512,512]{4,1,0,2,3:T(2,128)(2,1)} %copy.86), calls=%async_computation | async-start | bytes 8388608 | tf_op jit(solution)/shard_map/all_to_all | solution.py:46
  36.5 0.0 all-gather.3.cloned.1.call-start
  36.6 0.1 compare_select_fusion.2
  36.7 0.6 gather_fusion.2
  37.3 0.1 fusion.31
  37.4 0.1 add_bitcast_fusion
  37.5 10.1 %convolution_bitcast_fusion = f32[3,1024,512]{1,2,0:T(8,128)S(1)} fusion(bf16[3,2048,512]{2,1,0:T(8,128)(2,1)} %param.10, bf16[1024,2048,1]{1,0,2:T(8,128)(2,1)} %bitcast.61), kind=kOutput, calls=%fused_computation.16 | convolution fusion | flops 6442450944 | bytes 16777216 | tf_op jit(solution)/shard_map/rd,mdw->mrw/dot_general | solution.py:59
  47.6 2.6 copy-done.4
  50.2 1.1 slice.84
  51.3 1.8 convert_element_type.44
  53.2 1.1 copy.89
  54.3 5.0 %multiply_reduce_fusion.2 = (f32[1024]{0:T(1024)S(1)}, f32[1024]{0:T(1024)S(1)}, f32[1,1024,512]{1,2,0:T(8,128)}, f32[1,1024,512]{1,2,0:T(8,128)}) fusion(f32[3,1024,512]{1,2,0:T(8,128)} %copy-done.4), kind=kLoop, calls=%fused_computation.31 | loop fusion | flops 2095104 | bytes 8396800 | tf_op jit(solution)/shard_map/reduce_sum | solution.py:64
  59.4 32.4 %all-reduce = (f32[1024]{0:T(1024)S(1)}, f32[1024]{0:T(1024)S(1)}) all-reduce(f32[1024]{0:T(1024)S(1)} %get-tuple-element.18, f32[1024]{0:T(1024)S(1)} %get-tuple-element.17), channel_id=1, replica_groups=mesh['req'=32,'tensor'=4] {'tensor'}, use_global_device_ids=true, to_apply=%region_3.4 | all-reduce | flops 2048 | bytes 16384 | tf_op jit(solution)/shard_map/psum | solution.py:63
  91.8 1.0 multiply_cosine_fusion
  92.8 1.8 multiply_multiply_fusion.1
  94.6 0.2 multiply_multiply_fusion
  94.9 1.9 subtract_convert_fusion.1
  96.8 1.4 concatenate.29
  98.2 1.4 copy.90
  99.6 1.4 concatenate.30
  101.0 1.4 copy.91
  102.4 1.4 concatenate.33
  103.8 1.3 copy.94
  105.1 0.4 concatenate.32
  105.5 1.4 copy.93
  106.9 0.1 iota_compare_fusion
  107.0 0.1 iota_compare_fusion.1
  107.0 0.1 broadcast_in_dim.97
  107.2 0.1 broadcast_in_dim.96
  107.3 1.1 pad_add_fusion
  108.4 3.5 %fusion.32 = (bf16[1,2,1,512,512]{4,1,0,2,3:T(2,128)(2,1)S(1)}, bf16[1,2,1,512,512]{4,1,0,2,3:T(2,128)(2,1)}) fusion(bf16[4,2,1,512,512]{4,1,0,2,3:T(2,128)(2,1)} %all-to-all-done), kind=kLoop, calls=%fused_computation.70 | loop fusion | bytes 4194304 | tf_op jit(solution)/shard_map/slice | solution.py:83
  111.9 2.5 copy.87
  114.3 2.4 copy.99
  116.8 1.3 copy.95
  118.1 10.6 %fusion.9 = f32[2,4,512,1024]{3,2,1,0:T(8,128)} fusion(bf16[2,512,4,64]{3,1,2,0:T(8,128)(2,1)} %copy.94, bf16[2,512,4,64]{3,1,2,0:T(8,128)(2,1)} %copy.93, bf16[2,512,4,128]{3,1,2,0:T(8,128)(2,1)} %copy.95, bf16[2,512,4,64]{3,1,2,0:T(8,128)(2,1)} %copy.91, bf16[2,512,4,64]{3,1,2,0:T(8,128)(2,1)} %copy.90), kind=kOutput, calls=%fused_computation.21 | convolution fusion | flops 1082130432 | bytes 19922944 | tf_op jit(solution)/shard_map/bqhd,bkhd->bhqk/dot_general | solution.py:88
  128.7 22.1 %fusion.34 = (f32[2,4,512]{2,1,0:T(4,128)S(1)}, f32[2,4,512,1024]{3,2,1,0:T(8,128)}) fusion(f32[2,4,512,1024]{3,2,1,0:T(8,128)} %fusion.9, pred[2,512,1024]{2,1,0:T(8,128)(4,1)} %pad_add_fusion), kind=kOutput, calls=%fused_computation.72 | output fusion | flops 25166848 | bytes 34619392 | tf_op jit(solution)/shard_map/sub | solution.py:102
  150.8 8.5 %fusion.18 = bf16[2,512,4,128]{1,3,2,0:T(8,128)(2,1)} fusion(f32[2,4,512,1024]{3,2,1,0:T(8,128)} %get-tuple-element.38, f32[2,4,512]{2,1,0:T(4,128)S(1)} %get-tuple-element.37, bf16[2,512,4,128]{1,3,2,0:T(8,128)(2,1)S(1)} %copy-done.5, bf16[2,512,4,128]{1,3,2,0:T(8,128)(2,1)} %bitcast.59), kind=kOutput, calls=%fused_computation.33 | convolution fusion | flops 1086849024 | bytes 19939328 | tf_op jit(solution)/shard_map/bhqk,bkhd->bqhd/dot_general | solution.py:104
  159.3 1.7 copy.96
  161.0 4.3 %convolution_convert_fusion = bf16[1024,2048]{1,0:T(8,128)(2,1)} fusion(bf16[512,2048]{1,0:T(8,128)(2,1)S(1)} %copy-done, bf16[128,8,4,128]{3,2,1,0:T(4,128)(2,1)S(1)} %bitcast.60), kind=kOutput, calls=%fused_computation.15 | convolution fusion | flops 2149580800 | bytes 7340032 | tf_op jit(solution)/shard_map/dot_general | solution.py:108
  165.3 0.6 copy-done.8
  166.0 5.7 %copy.97 = bf16[4,2,512,512]{3,2,1,0:T(8,128)(2,1)} copy(bf16[4,2,512,512]{3,1,0,2:T(2,128)(2,1)} %bitcast.21) | data formatting | bytes 8388608
  171.7 144.9 %all-gather.3.cloned.1.call-done = bf16[4096,2048]{1,0:T(8,128)(2,1)} async-done(((bf16[1024,2048]{1,0:T(8,128)(2,1)}), bf16[4096,2048]{1,0:T(8,128)(2,1)}) %all-gather.3.cloned.1.call-update) | async-done | bytes 16777232 | tf_op jit(solution)/shard_map/all_gather | solution.py:116
  316.5 12.0 %reduce_sum.51 = bf16[1024,2048]{1,0:T(8,128)(2,1)} reduce(bf16[4,1024,2048]{2,1,0:T(8,128)(2,1)} %bitcast.53, bf16[]{:T(256)} %constant.96.clone.1), dimensions={0}, to_apply=%region_6.7 | reduce | flops 6291456 | bytes 20971522 | tf_op jit(solution)/shard_map/reduce_sum | solution.py:116
  328.6 3.2 multiply_reduce_fusion
  331.8 0.2 copy-done.2
  332.0 1.1 convert_element_type.51
  333.1 2.6 add_convert_fusion
  (31 shorter events, 0.2 us)
Async XLA Ops:
  7.2 153.9 %copy-start = (bf16[512,2048]{1,0:T(8,128)(2,1)S(1)}, bf16[512,2048]{1,0:T(8,128)(2,1)}, u32[]{:S(2)}) copy-start(bf16[512,2048]{1,0:T(8,128)(2,1)} %param.12) | copy-start | bytes 6291460
  24.9 11.7 %copy-start.7 = (s32[64]{0:T(128)S(1)}, s32[64]{0:T(128)}, u32[]{:S(2)}) copy-start(s32[64]{0:T(128)} %param.16) | copy-start | bytes 772
  24.9 11.8 %copy-start.1 = (s32[64]{0:T(128)S(1)}, s32[64]{0:T(128)}, u32[]{:S(2)}) copy-start(s32[64]{0:T(128)} %param.17) | copy-start | bytes 772
  24.9 83.5 %all-to-all-start = ((bf16[4,2,1,512,512]{4,1,0,2,3:T(2,128)(2,1)}), bf16[4,2,1,512,512]{4,1,0,2,3:T(2,128)(2,1)}, u32[]{:S(2)}, u32[]{:S(2)}) async-start(bf16[4,2,1,512,512]{4,1,0,2,3:T(2,128)(2,1)} %copy.86), calls=%async_computation | async-start | bytes 8388608 | tf_op jit(solution)/shard_map/all_to_all | solution.py:46
  36.5 280.0 %all-gather.3.cloned.1.call-start = ((), (), s32[]{:S(2)}) async-start(), calls=%async_computation.1 | async-start | bytes 20971520 | tf_op jit(solution)/shard_map/all_gather | solution.py:116
  47.6 2.6 copy-start.4
  54.3 37.4 %copy-start.6 = (bf16[2,512]{1,0:T(2,128)(2,1)S(1)}, bf16[2,512]{1,0:T(2,128)(2,1)}, u32[]{:S(2)}) copy-start(bf16[2,512]{1,0:T(2,128)(2,1)} %param.11) | copy-start | bytes 6148
  91.7 2.9 copy-start.3
  128.7 22.1 %copy-start.5 = (bf16[2,512,4,128]{1,3,2,0:T(8,128)(2,1)S(1)}, bf16[2,512,4,128]{1,3,2,0:T(8,128)(2,1)}, u32[]{:S(2)}) copy-start(bf16[2,512,4,128]{1,3,2,0:T(8,128)(2,1)} %copy.89) | copy-start | bytes 3145732
  165.3 0.7 copy-start.8
  328.6 3.4 %copy-start.2 = (bf16[1024,2048]{1,0:T(8,128)(2,1)S(1)}, bf16[1024,2048]{1,0:T(8,128)(2,1)}, u32[]{:S(2)}) copy-start(bf16[1024,2048]{1,0:T(8,128)(2,1)} %reduce_sum.51) | copy-start | bytes 12582916
Sparse Core Ops, SparseCore 0:
  165.5 151.0 all-gather.2
